TPU v7x, 32 devices: a whole 2x2x4 slice. The times are simulated.
32 devices in a mesh: traj: 8 (over z, core), amp: 4 (over y, x).
Axes of the slice: x: 2, y: 2, z: 4, core: 2. Of those that a mesh axis runs over, the one named last changes fastest.
Arguments:
- amplitudes: float32 [8, 2, 524288], P('traj', None, 'amp'), parts along dimension 0, may hold values from -6 to 6
- couplings: float32 [18], replicated, may hold values from 0.5 to 2
- fields: float32 [19], replicated, may hold values from 0.5 to 2
- decays: float32 [19], replicated, may hold values from 0.2 to 2
- channel: int32 [8], P('traj'), parts along dimension 0, may hold values from 0 to 19
Outputs:
- evolved_state: float32 [8, 2, 524288], P('traj', None, 'amp'), parts along dimension 0
There are 8 independent parts, one for each index of `traj`. A program takes and returns all parts, laid end to end along the dimension named above; an argument that names none is the same for every part. Nothing has to cross between parts.
Inputs may be any that keep to these rules, and one draw needn't show every extreme that they name: `channel`: the value 19 means that the trajectory does not jump.
All inputs are finite; a program needn't handle non-finite values.
Results may differ from a plain program's by a relative error of at most 0.0003.
Values sent between devices are 32-bit elements; how exact they have to be, the bound alone decides.
A program may use at most 256 MiB of HBM per device.

v0:
```python
import jax
import jax.numpy as jnp
from jax import lax
from jax.sharding import PartitionSpec as P

SPINS = 19
KRYLOV = 8


time_step = 0.7
squarings = 8
taylor_order = 10
highest = lax.Precision.HIGHEST


def partner_2(value, axis, distance):
    mask = 2**distance
    pairs = [(source, source ^ mask) for source in range(lax.axis_size(axis))]
    return lax.ppermute(value, axis, pairs)


def flip_axis(tensor, axis_pos, bit_pos):
    old_shape = tensor.shape
    new_shape = (
        old_shape[:axis_pos]
        + (old_shape[axis_pos] >> bit_pos + 1, 2, 1 << bit_pos)
        + old_shape[axis_pos + 1 :]
    )
    return jnp.flip(tensor.reshape(new_shape), axis=axis_pos + 1).reshape(old_shape)


def krylov_weights(scale_norm, hess_real, hess_imag):
    a_real = time_step * hess_imag
    a_imag = -time_step * hess_real
    upper_half = jnp.concatenate([a_real, -a_imag], axis=2)
    lower_half = jnp.concatenate([a_imag, a_real], axis=2)
    scaled = jnp.concatenate([upper_half, lower_half], axis=1) / 2.0**squarings
    identity = jnp.broadcast_to(jnp.eye(2 * KRYLOV, dtype=jnp.float32), scaled.shape)
    series = identity
    for degree in range(taylor_order, 0, -1):
        series = identity + jnp.einsum("tij,tjk->tik", scaled, series, precision=highest) / degree
    for repeat in range(squarings):
        series = jnp.einsum("tij,tjk->tik", series, series, precision=highest)
    first_column = series[:, :, 0] * scale_norm[:, None]
    return (first_column[:, :KRYLOV], first_column[:, KRYLOV:])


def projections(local_proj):
    return lax.psum(local_proj, "amp")


def subtract_span(applied, stacked, projected):
    proj_real = projected[:, :, 0]
    proj_imag = projected[:, :, 1]
    comb_real = jnp.einsum(
        "tk,tkrl->trl", proj_real, stacked[:, :, 0], precision=highest
    ) - jnp.einsum("tk,tkrl->trl", proj_imag, stacked[:, :, 1], precision=highest)
    comb_imag = jnp.einsum(
        "tk,tkrl->trl", proj_real, stacked[:, :, 1], precision=highest
    ) + jnp.einsum("tk,tkrl->trl", proj_imag, stacked[:, :, 0], precision=highest)
    return applied - jnp.stack([comb_real, comb_imag], axis=1)


def body(amplitudes, couplings, fields, decays, channel):
    node_count = lax.axis_size("amp")
    high_bits = node_count.bit_length() - 1
    device = lax.axis_index("amp")
    traj_count = amplitudes.shape[0]
    local_len = amplitudes.shape[2]
    row_count = local_len // 128
    block_len = local_len // node_count
    low_spins = SPINS - high_bits
    band_low = SPINS - 2 * high_bits
    local_ids = jnp.arange(local_len, dtype=jnp.int32)
    position = device * local_len + local_ids
    occupation = [(position >> spin_pos & 1).astype(jnp.float32) for spin_pos in range(SPINS)]
    diag_real = jnp.zeros((local_len,), jnp.float32)
    for spin_pos in range(SPINS - 1):
        diag_real = diag_real - couplings[spin_pos] * (1.0 - 2.0 * occupation[spin_pos]) * (
            1.0 - 2.0 * occupation[spin_pos + 1]
        )
    diag_imag = jnp.zeros((local_len,), jnp.float32)
    for spin_pos in range(SPINS):
        diag_imag = diag_imag - 0.5 * decays[spin_pos] * occupation[spin_pos]
    diag_real = diag_real.reshape(row_count, 128)
    diag_imag = diag_imag.reshape(row_count, 128)
    lane_ids = jnp.arange(128, dtype=jnp.int32)
    crossed = lane_ids[:, None] ^ lane_ids[None, :]
    lane_table = jnp.zeros((128, 128), jnp.float32)
    for spin_pos in range(7):
        lane_table = lane_table + fields[spin_pos] * (crossed == 1 << spin_pos).astype(jnp.float32)
    vector = amplitudes.reshape(traj_count, 2, row_count, 128)
    start_sq = lax.psum(jnp.sum(vector * vector, axis=(1, 2, 3)), "amp")
    scale_norm = jnp.sqrt(start_sq)
    krylov_basis = [vector / scale_norm[:, None, None, None]]
    hess_real = jnp.zeros((traj_count, KRYLOV, KRYLOV), jnp.float32)
    hess_imag = jnp.zeros((traj_count, KRYLOV, KRYLOV), jnp.float32)
    for column in range(KRYLOV):
        apply_vector = krylov_basis[column]
        flipped = jnp.einsum("tcrl,lm->tcrm", apply_vector, lane_table, precision=highest)
        for apply_spin_pos in range(7, low_spins):
            flipped = flipped + fields[apply_spin_pos] * flip_axis(
                apply_vector, 2, apply_spin_pos - 7
            )
        for apply_bit_pos in range(high_bits):
            partner = partner_2(apply_vector, "amp", apply_bit_pos)
            flipped = flipped + fields[low_spins + apply_bit_pos] * partner
        real_part = apply_vector[:, 0]
        imag_part = apply_vector[:, 1]
        out_real = diag_real * real_part - diag_imag * imag_part - flipped[:, 0]
        out_imag = diag_real * imag_part + diag_imag * real_part - flipped[:, 1]
        applied = jnp.stack([out_real, out_imag], axis=1)
        stacked = jnp.stack(krylov_basis, axis=1)
        swapped = jnp.stack([applied[:, 1], -applied[:, 0]], axis=1)
        paired = jnp.stack([applied, swapped], axis=1)
        local_proj = jnp.einsum("tkcrl,tpcrl->tkp", stacked, paired, precision=highest)
        if column + 1 == KRYLOV:
            projected = projections(local_proj)
        else:
            local_sq = jnp.sum(applied * applied, axis=(1, 2, 3))
            projected, whole_sq = lax.psum((local_proj, local_sq), "amp")
            residual = subtract_span(applied, stacked, projected)
            squares = whole_sq - jnp.sum(projected * projected, axis=(1, 2))
            column_norm = jnp.sqrt(squares)
            hess_real = hess_real.at[:, column + 1, column].set(column_norm)
            krylov_basis.append(residual / column_norm[:, None, None, None])
        hess_real = hess_real.at[:, : column + 1, column].set(projected[:, :, 0])
        hess_imag = hess_imag.at[:, : column + 1, column].set(projected[:, :, 1])
    weights_real, weights_imag = krylov_weights(scale_norm, hess_real, hess_imag)
    stacked = jnp.stack(krylov_basis, axis=1)
    new_real = jnp.einsum(
        "tk,tkrl->trl", weights_real, stacked[:, :, 0], precision=highest
    ) - jnp.einsum("tk,tkrl->trl", weights_imag, stacked[:, :, 1], precision=highest)
    new_imag = jnp.einsum(
        "tk,tkrl->trl", weights_real, stacked[:, :, 1], precision=highest
    ) + jnp.einsum("tk,tkrl->trl", weights_imag, stacked[:, :, 0], precision=highest)
    propagated = jnp.stack([new_real, new_imag], axis=1)
    lowered_local = jnp.zeros_like(propagated)
    for spin_pos in range(band_low, low_spins):
        vacant = (local_ids >> spin_pos & 1 == 0).reshape(row_count, 128)
        lowered_term = jnp.where(vacant, flip_axis(propagated, 2, spin_pos - 7), 0.0)
        lowered_local = jnp.where(
            (channel == spin_pos)[:, None, None, None], lowered_term, lowered_local
        )
    spread = propagated.reshape(traj_count, 2, node_count, block_len)
    relaid = lax.all_to_all(spread, "amp", split_axis=2, concat_axis=2, tiled=True)
    sources = jnp.arange(node_count, dtype=jnp.int32)
    offsets = jnp.arange(block_len, dtype=jnp.int32)
    lowered_relaid = jnp.zeros_like(relaid)
    for spin_pos in range(band_low):
        vacant = offsets >> spin_pos & 1 == 0
        lowered_term = jnp.where(vacant, flip_axis(relaid, 3, spin_pos), 0.0)
        lowered_relaid = jnp.where(
            (channel == spin_pos)[:, None, None, None], lowered_term, lowered_relaid
        )
    for bit_pos in range(high_bits):
        vacant = sources >> bit_pos & 1 == 0
        lowered_term = jnp.where(vacant[:, None], flip_axis(relaid, 2, bit_pos), 0.0)
        lowered_relaid = jnp.where(
            (channel == low_spins + bit_pos)[:, None, None, None], lowered_term, lowered_relaid
        )
    returned = lax.all_to_all(
        lowered_relaid, "amp", split_axis=2, concat_axis=2, tiled=True
    ).reshape(propagated.shape)
    in_band = (channel >= band_low) & (channel < low_spins)
    lowered = jnp.where(in_band[:, None, None, None], lowered_local, returned)
    jumped = channel < SPINS
    squared_sum = lax.psum(jnp.sum(lowered * lowered, axis=(1, 2, 3)), "amp")
    squared_sum = jnp.where(jumped, squared_sum, jnp.float32(local_len * node_count))
    lowered = lowered * jnp.sqrt(local_len * node_count / squared_sum)[:, None, None, None]
    result = jnp.where(jumped[:, None, None, None], lowered, propagated)
    return result.reshape(traj_count, 2, local_len)


def solution(mesh):
    placed = (P("traj", None, "amp"), P(), P(), P(), P("traj"))
    return jax.shard_map(
        body, mesh=mesh, in_specs=placed, out_specs=P("traj", None, "amp"), check_vma=False
    )
```

profile of v0, /device:TPU:0, one launch (start us, length us, event | category | flops | bytes accessed | tf_op | source)
XLA Modules:
  0.0 2174.6 jit_solution(13857305890439002905)
XLA Ops:
  2.9 12.0 psum.119
  78.8 11.4 multiply_add_fusion.7
  90.2 15.1 slice_subtract_fusion.14
  105.3 14.6 fusion.378
  121.4 10.5 all-reduce.8
  180.8 9.5 fusion.125
  193.2 15.8 slice_subtract_fusion.12
  209.0 15.7 fusion.377
  231.1 20.7 convolution_bitcast_fusion.7
  251.8 11.2 all-reduce.7
  340.6 9.5 fusion.120
  353.1 15.6 slice_subtract_fusion.10
  368.7 15.7 fusion.376
  390.9 21.1 convolution_bitcast_fusion.6
  412.0 11.0 all-reduce.6
  504.9 9.2 fusion.115
  517.1 15.6 slice_subtract_fusion.8
  532.7 15.7 fusion.375
  551.8 21.2 convolution_bitcast_fusion.5
  573.0 11.0 all-reduce.5
  678.1 14.6 slice_subtract_fusion.6
  692.7 14.8 fusion.374
  712.8 21.3 convolution_bitcast_fusion.4
  734.0 11.2 all-reduce.4
  756.7 8.9 fusion.6
  774.0 8.6 fusion.2
  843.6 14.6 slice_subtract_fusion.4
  858.2 14.6 fusion.373
  878.2 21.5 convolution_bitcast_fusion.3
  899.7 11.1 all-reduce.3
  923.3 8.6 fusion.14
  940.5 8.7 fusion.10
  980.5 8.6 copy.117
  1009.8 14.6 slice_subtract_fusion.2
  1024.4 14.6 fusion.367
  1044.3 21.7 convolution_bitcast_fusion.2
  1066.1 11.2 all-reduce.2
  1089.9 8.7 fusion.22
  1107.0 8.7 fusion.18
  1152.1 9.3 copy.120
  1163.5 9.5 fusion.95
  1176.0 14.6 slice_subtract_fusion
  1190.6 14.6 fusion.366
  1209.7 20.6 convolution_bitcast_fusion.1
  1231.8 10.4 psum.134
  1253.7 8.7 fusion.30
  1270.8 8.9 fusion.26
  1296.1 66.1 %reshape.8754 = f32[1,2,4,4096,2,4]{5,4,3,2,1,0:T(2,128)} reshape(f32[1,2,4,32768]{3,2,1,0:T(4,128)S(1)} %copy.136) | data formatting | bytes 2097152 | tf_op jit(solution)/shard_map/reshape | solution.py:29
  1362.2 32.7 %reshape.8752 = f32[1,2,4,2048,2,8]{5,4,3,2,1,0:T(2,128)} reshape(f32[1,2,4,32768]{3,2,1,0:T(4,128)S(1)} %copy.136) | data formatting | bytes 2097152 | tf_op jit(solution)/shard_map/reshape | solution.py:29
  1394.9 13.1 reshape.8750
  1417.9 16.4 copy.141
  1434.3 156.0 %rev.422 = f32[1,2,4,16384,2,1]{2,4,3,1,5,0:T(2,128)} reverse(f32[1,2,4,16384,2,1]{2,4,3,1,5,0:T(2,128)} %bitcast.1047), dimensions={4} | reverse | bytes 2097152 | tf_op jit(solution)/shard_map/jit(_flip)/rev | solution.py:29
  1590.2 18.3 copy.144
  1608.5 23.3 %rev.421 = f32[1,2,4,8192,2,2]{2,5,4,3,1,0:T(2,128)} reverse(f32[1,2,4,8192,2,2]{2,5,4,3,1,0:T(2,128)} %bitcast.1048), dimensions={4} | reverse | bytes 2097152 | tf_op jit(solution)/shard_map/jit(_flip)/rev | solution.py:29
  1631.8 18.3 copy.142
  1650.1 155.9 %rev.420 = f32[1,2,4,4096,2,4]{5,4,3,2,1,0:T(2,128)} reverse(f32[1,2,4,4096,2,4]{5,4,3,2,1,0:T(2,128)} %reshape.8754), dimensions={4} | reverse | bytes 2097152 | tf_op jit(solution)/shard_map/jit(_flip)/rev | solution.py:29
  1806.0 62.0 %reshape.8755 = f32[1,2,4,32768]{3,2,1,0:T(4,128)} reshape(f32[1,2,4,4096,2,4]{5,4,3,2,1,0:T(2,128)} %rev.420) | data formatting | bytes 2097152 | tf_op jit(solution)/shard_map/reshape | solution.py:29
  1868.0 78.5 %rev.419 = f32[1,2,4,2048,2,8]{5,4,3,2,1,0:T(2,128)} reverse(f32[1,2,4,2048,2,8]{5,4,3,2,1,0:T(2,128)} %reshape.8752), dimensions={4} | reverse | bytes 2097152 | tf_op jit(solution)/shard_map/jit(_flip)/rev | solution.py:29
  1946.5 35.0 %reshape.8753 = f32[1,2,4,32768]{3,2,1,0:T(4,128)} reshape(f32[1,2,4,2048,2,8]{5,4,3,2,1,0:T(2,128)} %rev.419) | data formatting | bytes 2097152 | tf_op jit(solution)/shard_map/reshape | solution.py:29
  1981.5 39.9 %rev.418 = f32[1,2,4,1024,2,16]{5,4,3,2,1,0:T(2,128)} reverse(f32[1,2,4,1024,2,16]{5,4,3,2,1,0:T(2,128)} %reshape.8750), dimensions={4} | reverse | bytes 2097152 | tf_op jit(solution)/shard_map/jit(_flip)/rev | solution.py:29
  2021.4 14.3 reshape.8751
  2035.6 20.6 rev.417
  2128.3 9.2 fusion.212
  2158.3 11.0 psum.135
  (635 shorter events, 753.3 us)
Async XLA Ops:
  17.3 61.5 %collective-permute-start.1 = (f32[1,2,1024,128]{3,2,1,0:T(8,128)S(1)}, f32[1,2,1024,128]{3,2,1,0:T(8,128)}, u32[]{:S(2)}, u32[]{:S(2)}) collective-permute-start(f32[1,2,1024,128]{3,2,1,0:T(8,128)S(1)} %copy.306), channel_id=1, source_target_pairs={{0,2},{1,3},{2,0},{3,1},{4,6},{5,7},{6,4},{7,5},{8,10},{9,11},{10,... | collective-permute-start | bytes 3145736 | tf_op jit(solution)/shard_map/ppermute | solution.py:19
  17.9 60.9 %collective-permute-start = (f32[1,2,1024,128]{3,2,1,0:T(8,128)S(1)}, f32[1,2,1024,128]{3,2,1,0:T(8,128)}, u32[]{:S(2)}, u32[]{:S(2)}) collective-permute-start(f32[1,2,1024,128]{3,2,1,0:T(8,128)S(1)} %copy.306), channel_id=1, source_target_pairs={{0,1},{1,0},{2,3},{3,2},{4,5},{5,4},{6,7},{7,6},{8,9},{9,8},{10,11... | collective-permute-start | bytes 3145736 | tf_op jit(solution)/shard_map/ppermute | solution.py:19
  20.8 9.5 copy-start.67
  22.9 14.2 copy-start.69
  22.9 14.9 copy-start.68
  22.9 17.6 copy-start.87
  22.9 18.3 copy-start.88
  22.9 19.7 copy-start.86
  22.9 21.1 copy-start.85
  22.9 22.4 %copy-start.84 = (s32[3]{0:T(128)S(1)}, s32[3]{0:T(128)}, u32[]{:S(2)}) copy-start(s32[3]{0:T(128)} %constant.807.clone.1) | copy-start | bytes 40
  58.8 20.0 copy-start.18
  136.9 53.3 %collective-permute-start.3 = (f32[1,2,1024,128]{3,2,1,0:T(8,128)}, f32[1,2,1024,128]{3,2,1,0:T(8,128)}, u32[]{:S(2)}, u32[]{:S(2)}) collective-permute-start(f32[1,2,1024,128]{3,2,1,0:T(8,128)} %fusion.146), channel_id=1, source_target_pairs={{0,2},{1,3},{2,0},{3,1},{4,6},{5,7},{6,4},{7,5},{8,10},{9,11},{10,... | collective-permute-start | bytes 3145736 | tf_op jit(solution)/shard_map/ppermute | solution.py:19
  137.5 52.7 %collective-permute-start.2 = (f32[1,2,1024,128]{3,2,1,0:T(8,128)}, f32[1,2,1024,128]{3,2,1,0:T(8,128)}, u32[]{:S(2)}, u32[]{:S(2)}) collective-permute-start(f32[1,2,1024,128]{3,2,1,0:T(8,128)} %fusion.146), channel_id=1, source_target_pairs={{0,1},{1,0},{2,3},{3,2},{4,5},{5,4},{6,7},{7,6},{8,9},{9,8},{10,11... | collective-permute-start | bytes 3145736 | tf_op jit(solution)/shard_map/ppermute | solution.py:19
  231.1 32.7 %copy-start.64 = (f32[2,1024,128]{2,1,0:T(8,128)S(1)}, f32[2,1024,128]{2,1,0:T(8,128)}, u32[]{:S(2)}) copy-start(f32[2,1024,128]{2,1,0:T(8,128)} %get-tuple-element.352) | copy-start | bytes 3145732
  291.2 58.9 %collective-permute-start.5 = (f32[1,2,1024,128]{3,2,1,0:T(8,128)}, f32[1,2,1024,128]{3,2,1,0:T(8,128)}, u32[]{:S(2)}, u32[]{:S(2)}) collective-permute-start(f32[1,2,1024,128]{3,2,1,0:T(8,128)} %fusion.155), channel_id=1, source_target_pairs={{0,2},{1,3},{2,0},{3,1},{4,6},{5,7},{6,4},{7,5},{8,10},{9,11},{10,... | collective-permute-start | bytes 3145736 | tf_op jit(solution)/shard_map/ppermute | solution.py:19
  291.8 58.3 %collective-permute-start.4 = (f32[1,2,1024,128]{3,2,1,0:T(8,128)}, f32[1,2,1024,128]{3,2,1,0:T(8,128)}, u32[]{:S(2)}, u32[]{:S(2)}) collective-permute-start(f32[1,2,1024,128]{3,2,1,0:T(8,128)} %fusion.155), channel_id=1, source_target_pairs={{0,1},{1,0},{2,3},{3,2},{4,5},{5,4},{6,7},{7,6},{8,9},{9,8},{10,11... | collective-permute-start | bytes 3145736 | tf_op jit(solution)/shard_map/ppermute | solution.py:19
  425.4 14.5 copy-start.14
  425.4 22.3 %copy-start.13 = (f32[3,1024,128]{2,1,0:T(8,128)S(1)}, f32[3,1024,128]{2,1,0:T(8,128)}, u32[]{:S(2)}) copy-start(f32[3,1024,128]{2,1,0:T(8,128)} %get-tuple-element.346) | copy-start | bytes 4718596
  456.3 57.9 %collective-permute-start.7 = (f32[1,2,1024,128]{3,2,1,0:T(8,128)}, f32[1,2,1024,128]{3,2,1,0:T(8,128)}, u32[]{:S(2)}, u32[]{:S(2)}) collective-permute-start(f32[1,2,1024,128]{3,2,1,0:T(8,128)} %fusion.164), channel_id=1, source_target_pairs={{0,2},{1,3},{2,0},{3,1},{4,6},{5,7},{6,4},{7,5},{8,10},{9,11},{10,... | collective-permute-start | bytes 3145736 | tf_op jit(solution)/shard_map/ppermute | solution.py:19
  456.9 57.3 %collective-permute-start.6 = (f32[1,2,1024,128]{3,2,1,0:T(8,128)}, f32[1,2,1024,128]{3,2,1,0:T(8,128)}, u32[]{:S(2)}, u32[]{:S(2)}) collective-permute-start(f32[1,2,1024,128]{3,2,1,0:T(8,128)} %fusion.164), channel_id=1, source_target_pairs={{0,1},{1,0},{2,3},{3,2},{4,5},{5,4},{6,7},{7,6},{8,9},{9,8},{10,11... | collective-permute-start | bytes 3145736 | tf_op jit(solution)/shard_map/ppermute | solution.py:19
  493.9 11.0 copy-start.32
  551.8 36.7 %copy-start.15 = (f32[4,1024,128]{2,1,0:T(8,128)S(1)}, f32[4,1024,128]{2,1,0:T(8,128)}, u32[]{:S(2)}) copy-start(f32[4,1024,128]{2,1,0:T(8,128)} %get-tuple-element.342) | copy-start | bytes 6291460
  586.2 16.4 copy-start.16
  618.2 56.9 %collective-permute-start.9 = (f32[1,2,1024,128]{3,2,1,0:T(8,128)S(1)}, f32[1,2,1024,128]{3,2,1,0:T(8,128)}, u32[]{:S(2)}, u32[]{:S(2)}) collective-permute-start(f32[1,2,1024,128]{3,2,1,0:T(8,128)S(1)} %fusion.173), channel_id=1, source_target_pairs={{0,2},{1,3},{2,0},{3,1},{4,6},{5,7},{6,4},{7,5},{8,10},{9,11},{10,... | collective-permute-start | bytes 3145736 | tf_op jit(solution)/shard_map/ppermute | solution.py:19
  618.9 56.3 %collective-permute-start.8 = (f32[1,2,1024,128]{3,2,1,0:T(8,128)S(1)}, f32[1,2,1024,128]{3,2,1,0:T(8,128)}, u32[]{:S(2)}, u32[]{:S(2)}) collective-permute-start(f32[1,2,1024,128]{3,2,1,0:T(8,128)S(1)} %fusion.173), channel_id=1, source_target_pairs={{0,1},{1,0},{2,3},{3,2},{4,5},{5,4},{6,7},{7,6},{8,9},{9,8},{10,11... | collective-permute-start | bytes 3145736 | tf_op jit(solution)/shard_map/ppermute | solution.py:19
  747.4 9.3 copy-start.1
  756.7 17.4 copy-start
  782.9 57.8 %collective-permute-start.11 = (f32[1,2,1024,128]{3,2,1,0:T(8,128)S(1)}, f32[1,2,1024,128]{3,2,1,0:T(8,128)}, u32[]{:S(2)}, u32[]{:S(2)}) collective-permute-start(f32[1,2,1024,128]{3,2,1,0:T(8,128)S(1)} %fusion.182), channel_id=1, source_target_pairs={{0,2},{1,3},{2,0},{3,1},{4,6},{5,7},{6,4},{7,5},{8,10},{9,11},{10,... | collective-permute-start | bytes 3145736 | tf_op jit(solution)/shard_map/ppermute | solution.py:19
  783.5 57.1 %collective-permute-start.10 = (f32[1,2,1024,128]{3,2,1,0:T(8,128)S(1)}, f32[1,2,1024,128]{3,2,1,0:T(8,128)}, u32[]{:S(2)}, u32[]{:S(2)}) collective-permute-start(f32[1,2,1024,128]{3,2,1,0:T(8,128)S(1)} %fusion.182), channel_id=1, source_target_pairs={{0,1},{1,0},{2,3},{3,2},{4,5},{5,4},{6,7},{7,6},{8,9},{9,8},{10,11... | collective-permute-start | bytes 3145736 | tf_op jit(solution)/shard_map/ppermute | solution.py:19
  826.9 7.8 copy-start.54
  826.9 8.1 copy-start.59
  913.5 9.8 copy-start.3
  923.3 17.1 copy-start.2
  949.4 57.5 %collective-permute-start.13 = (f32[1,2,1024,128]{3,2,1,0:T(8,128)S(1)}, f32[1,2,1024,128]{3,2,1,0:T(8,128)}, u32[]{:S(2)}, u32[]{:S(2)}) collective-permute-start(f32[1,2,1024,128]{3,2,1,0:T(8,128)S(1)} %fusion.191), channel_id=1, source_target_pairs={{0,2},{1,3},{2,0},{3,1},{4,6},{5,7},{6,4},{7,5},{8,10},{9,11},{10,... | collective-permute-start | bytes 3145736 | tf_op jit(solution)/shard_map/ppermute | solution.py:19
  950.0 56.9 %collective-permute-start.12 = (f32[1,2,1024,128]{3,2,1,0:T(8,128)S(1)}, f32[1,2,1024,128]{3,2,1,0:T(8,128)}, u32[]{:S(2)}, u32[]{:S(2)}) collective-permute-start(f32[1,2,1024,128]{3,2,1,0:T(8,128)S(1)} %fusion.191), channel_id=1, source_target_pairs={{0,1},{1,0},{2,3},{3,2},{4,5},{5,4},{6,7},{7,6},{8,9},{9,8},{10,11... | collective-permute-start | bytes 3145736 | tf_op jit(solution)/shard_map/ppermute | solution.py:19
  992.4 7.7 copy-start.37
  992.4 7.7 copy-start.40
  992.5 8.0 copy-start.56
  992.5 8.7 copy-start.57
  1079.6 10.3 copy-start.5
  1089.9 17.2 copy-start.4
  1098.5 18.1 slice-start
  1107.0 9.6 slice-start.1
  1116.0 57.0 %collective-permute-start.15 = (f32[1,2,1024,128]{3,2,1,0:T(8,128)S(1)}, f32[1,2,1024,128]{3,2,1,0:T(8,128)}, u32[]{:S(2)}, u32[]{:S(2)}) collective-permute-start(f32[1,2,1024,128]{3,2,1,0:T(8,128)S(1)} %fusion.201), channel_id=1, source_target_pairs={{0,2},{1,3},{2,0},{3,1},{4,6},{5,7},{6,4},{7,5},{8,10},{9,11},{10,... | collective-permute-start | bytes 3145736 | tf_op jit(solution)/shard_map/ppermute | solution.py:19
  1116.6 56.4 %collective-permute-start.14 = (f32[1,2,1024,128]{3,2,1,0:T(8,128)S(1)}, f32[1,2,1024,128]{3,2,1,0:T(8,128)}, u32[]{:S(2)}, u32[]{:S(2)}) collective-permute-start(f32[1,2,1024,128]{3,2,1,0:T(8,128)S(1)} %fusion.201), channel_id=1, source_target_pairs={{0,1},{1,0},{2,3},{3,2},{4,5},{5,4},{6,7},{7,6},{8,9},{9,8},{10,11... | collective-permute-start | bytes 3145736 | tf_op jit(solution)/shard_map/ppermute | solution.py:19
  1242.7 11.0 copy-start.12
  1245.4 17.0 copy-start.11
  1282.3 13.1 all-to-all-start
  2120.3 7.9 copy-start.63
  2120.3 7.9 copy-start.70
  2120.3 7.9 copy-start.71
  2120.3 7.9 copy-start.72
  2120.4 7.9 copy-start.73
  2120.4 7.9 copy-start.74
  2120.4 7.9 copy-start.75
  2120.4 7.9 copy-start.76
  2120.4 7.9 copy-start.77
  2120.4 7.9 copy-start.78
  2120.4 7.9 copy-start.79
  2120.4 7.9 copy-start.80
  2120.4 7.9 copy-start.81
  2120.4 7.9 copy-start.82
  2120.5 7.9 copy-start.83
  2139.4 15.6 all-to-all-start.1
  (45 other events, 260.8 us)
where the time goes:
time: 2200 us; the launch traced here: 2170 us
  local copies, waits for them, and re-layouts  1050 us (48%)
  other arithmetic  535 us (24%)
  matrix products  433 us (20%)
  blocking collectives  110 us (5%)
  between operations  25.7 us (1%)
    rev x19, local copies, waits for them, and re-layouts, flip_axis(): jnp.flip(tensor.reshape(new_shape), axis=axis_pos + 1).reshape(old_shape)  514 us
    reshape x19, local copies, waits for them, and re-layouts, flip_axis(): jnp.flip(tensor.reshape(new_shape), axis=axis_pos + 1).reshape(old_shape)  180 us
    another operation x35, local copies, waits for them, and re-layouts  154 us
    mul x80, other arithmetic, body(): fields[apply_spin_pos] * flip_axis(apply_vector, 2, apply_spin_pos - 7)  150 us
    dot_general x7, matrix products, body(): jnp.einsum('tkcrl,tpcrl->tkp', stacked, paired, precision=highest)  148 us
    reshape x21, local copies, waits for them, and re-layouts, flip_axis(): tensor.reshape(new_shape)  131 us
    sub x8, other arithmetic, body(): out_imag = diag_real * imag_part + diag_imag * real_part - flipped[:, 1]  120 us
    neg x8, other arithmetic, body(): swapped = jnp.stack([applied[:, 1], -applied[:, 0]], axis=1)  120 us
  transfers between devices with their start and end apart: 18, of which 1 were waited for; matrix products, arithmetic and copies ran while one was open for 21% of the time, Pallas kernels for 0%

commit v1 on v0

v1 whole, which is shorter than its diff:
```python
import jax
import jax.numpy as jnp
from jax import lax
from jax.experimental import pallas as pl
from jax.experimental.pallas import tpu as pltpu
from jax.sharding import PartitionSpec as P

SPINS = 19
KRYLOV = 8
LANES = 128
LANE_BITS = 7

time_step = 0.7
squarings = 8
taylor_order = 10
highest = lax.Precision.HIGHEST

CHUNK_BITS = 8
CHUNK = 1 << CHUNK_BITS
SUB = 32


def split(x):
    hi = x.astype(jnp.bfloat16)
    lo = (x - hi.astype(jnp.float32)).astype(jnp.bfloat16)
    return hi, lo


def dot(a, b):
    return jnp.dot(a, b, preferred_element_type=jnp.float32)


def fold(x):
    return jnp.sum(x.reshape(x.shape[0] // 8, 8, x.shape[1]), axis=0)


def scalar_sqrt(value):
    root = jnp.sqrt(jnp.full((8, LANES), value, jnp.float32))
    return jnp.max(root), jnp.max(1.0 / root)


def krylov_weights(a_matrix):
    size = a_matrix.shape[0]
    pad = jnp.zeros((LANES - size, LANES), jnp.float32)
    scaled = jnp.concatenate([a_matrix, pad], axis=0) * (1.0 / 2.0**squarings)
    rows = lax.broadcasted_iota(jnp.int32, (LANES, LANES), 0)
    cols = lax.broadcasted_iota(jnp.int32, (LANES, LANES), 1)
    identity = jnp.where(rows == cols, 1.0, 0.0).astype(jnp.float32)
    series = identity
    for degree in range(taylor_order, 0, -1):
        product = jnp.dot(
            scaled, series, precision=highest, preferred_element_type=jnp.float32
        )
        series = identity + product * (1.0 / degree)
    for repeat in range(squarings):
        series = jnp.dot(
            series, series, precision=highest, preferred_element_type=jnp.float32
        )
    return series


def kernel(
    channel_ref,
    couplings,
    fields,
    decays,
    state,
    out,
    basis,
    work,
    flips,
    row_table,
    lane_table,
    diag_low,
):
    node_count, _, block_rows, _ = state.shape
    rows = node_count * block_rows
    chunks = rows // CHUNK
    subs = CHUNK // SUB
    channel = channel_ref[0]
    device = lax.axis_index("amp")
    zero_tile = jnp.zeros((8, LANES), jnp.float32)
    per_block = block_rows // CHUNK

    table_shape = (CHUNK, CHUNK)
    crossed = lax.broadcasted_iota(jnp.int32, table_shape, 0)
    crossed = crossed ^ lax.broadcasted_iota(jnp.int32, table_shape, 1)
    for table, first_spin, bits in (
        (row_table, LANE_BITS, CHUNK_BITS),
        (lane_table, 0, LANE_BITS),
    ):
        value = jnp.zeros(table_shape, jnp.float32)
        for bit in range(bits):
            value = jnp.where(crossed == 1 << bit, fields[first_spin + bit], value)
        table[0], table[1] = split(value)

    low_shape = (CHUNK, LANES)
    low_pos = lax.broadcasted_iota(jnp.int32, low_shape, 0) * LANES
    low_pos = low_pos + lax.broadcasted_iota(jnp.int32, low_shape, 1)
    low_bits = LANE_BITS + CHUNK_BITS
    before = None
    low_real = jnp.zeros(low_shape, jnp.float32)
    low_imag = jnp.zeros(low_shape, jnp.float32)
    for spin in range(low_bits):
        occupied = (lax.shift_right_logical(low_pos, spin) & 1).astype(jnp.float32)
        sign = 1.0 - 2.0 * occupied
        low_imag = low_imag - 0.5 * decays[spin] * occupied
        if spin > 0:
            low_real = low_real - couplings[spin - 1] * (before * sign)
        before = sign
    diag_low[0] = low_real
    diag_low[1] = low_imag

    def high_diagonal(i):
        bits = [
            (lax.shift_right_logical(i, b) & 1).astype(jnp.float32)
            for b in range(SPINS - low_bits)
        ]
        signs = [1.0 - 2.0 * bit for bit in bits]
        real = jnp.float32(0.0)
        imag = jnp.float32(0.0)
        for b in range(len(bits)):
            imag = imag - 0.5 * decays[low_bits + b] * bits[b]
            if b > 0:
                real = real - couplings[low_bits + b - 1] * signs[b - 1] * signs[b]
        edge = couplings[low_bits - 1] * signs[0]
        return real - edge, real + edge, imag

    def start_norm(i, acc):
        node = i // per_block
        first = (i % per_block) * CHUNK
        for part in range(2):
            x = state[node, part, pl.ds(first, CHUNK), :]
            acc = acc + fold(x * x)
        return acc

    start_sq = jnp.sum(lax.fori_loop(0, chunks, start_norm, zero_tile))
    beta, inv_beta = scalar_sqrt(start_sq)

    def start_vector(i, carry):
        node = i // per_block
        first = (i % per_block) * CHUNK
        for part in range(2):
            basis[0, pl.ds(i * CHUNK, CHUNK), part * LANES : (part + 1) * LANES] = (
                state[node, part, pl.ds(first, CHUNK), :] * inv_beta
            )
        return carry

    lax.fori_loop(0, chunks, start_vector, 0)

    mat_rows = lax.broadcasted_iota(jnp.int32, (2 * KRYLOV, LANES), 0)
    mat_cols = lax.broadcasted_iota(jnp.int32, (2 * KRYLOV, LANES), 1)
    a_matrix = jnp.zeros((2 * KRYLOV, LANES), jnp.float32)

    def put(matrix, k, j, real, imag):
        a_real = time_step * imag
        a_imag = -time_step * real
        for r, c, value in (
            (k, j, a_real),
            (k, j + KRYLOV, -a_imag),
            (k + KRYLOV, j, a_imag),
            (k + KRYLOV, j + KRYLOV, a_real),
        ):
            matrix = jnp.where((mat_rows == r) & (mat_cols == c), value, matrix)
        return matrix

    high_fields = [
        fields[LANE_BITS + CHUNK_BITS + b] for b in range(SPINS - LANE_BITS - CHUNK_BITS)
    ]

    for j in range(KRYLOV):
        last = j + 1 == KRYLOV

        def apply_chunk(i, acc, j=j):
            base = pl.multiple_of(i * CHUNK, CHUNK)
            hi, lo = split(basis[j, pl.ds(base, CHUNK), :])
            flips[...] = (
                dot(row_table[0], hi)
                + dot(row_table[1], hi)
                + dot(row_table[0], lo)
                + dot(hi, lane_table[0])
                + dot(lo, lane_table[0])
                + dot(hi, lane_table[1])
            )
            acc = list(acc)
            real_vacant, real_occupied, imag_high = high_diagonal(i)
            for s in range(subs):
                here = pl.ds(base + s * SUB, SUB)
                x = basis[j, here, :]
                f = flips[s * SUB : (s + 1) * SUB, :]
                for b, field in enumerate(high_fields):
                    there = pl.multiple_of((i ^ (1 << b)) * CHUNK, CHUNK)
                    f = f + field * basis[j, pl.ds(there + s * SUB, SUB), :]
                part = slice(s * SUB, (s + 1) * SUB)
                dr = diag_low[0, part, :] + (real_vacant if s < subs // 2 else real_occupied)
                di = diag_low[1, part, :] + imag_high
                xr, xi = x[:, :LANES], x[:, LANES:]
                wr = dr * xr - di * xi - f[:, :LANES]
                wi = dr * xi + di * xr - f[:, LANES:]
                work[here, :LANES] = wr
                work[here, LANES:] = wi
                for k in range(j + 1):
                    vr = basis[k, here, :LANES]
                    vi = basis[k, here, LANES:]
                    acc[2 * k] = acc[2 * k] + fold(vr * wr + vi * wi)
                    acc[2 * k + 1] = acc[2 * k + 1] + fold(vr * wi - vi * wr)
                acc[-1] = acc[-1] + fold(wr * wr + wi * wi)
            return tuple(acc)

        sums = lax.fori_loop(0, chunks, apply_chunk, (zero_tile,) * (2 * j + 3))
        coeffs = [jnp.sum(t) for t in sums]
        for k in range(j + 1):
            a_matrix = put(a_matrix, k, j, coeffs[2 * k], coeffs[2 * k + 1])
        if last:
            break
        left = coeffs[-1]
        for value in coeffs[:-1]:
            left = left - value * value
        norm, inv_norm = scalar_sqrt(left)
        a_matrix = put(a_matrix, j + 1, j, norm, jnp.float32(0.0))

        def subtract_chunk(i, carry, j=j, coeffs=coeffs, inv_norm=inv_norm):
            base = pl.multiple_of(i * CHUNK, CHUNK)
            for s in range(subs):
                here = pl.ds(base + s * SUB, SUB)
                rr = work[here, :LANES]
                ri = work[here, LANES:]
                for k in range(j + 1):
                    vr = basis[k, here, :LANES]
                    vi = basis[k, here, LANES:]
                    hr, hm = coeffs[2 * k], coeffs[2 * k + 1]
                    rr = rr - (hr * vr - hm * vi)
                    ri = ri - (hr * vi + hm * vr)
                basis[j + 1, here, :LANES] = rr * inv_norm
                basis[j + 1, here, LANES:] = ri * inv_norm
            return carry

        lax.fori_loop(0, chunks, subtract_chunk, 0)

    series = krylov_weights(a_matrix)
    first = series[: 2 * KRYLOV, :] * beta
    weights = [
        jnp.sum(jnp.where((mat_rows == k) & (mat_cols == 0), first, 0.0))
        for k in range(2 * KRYLOV)
    ]
    sub_pos = lax.broadcasted_iota(jnp.int32, (SUB, LANES), 0) * LANES
    sub_pos = sub_pos + lax.broadcasted_iota(jnp.int32, (SUB, LANES), 1)

    def combine(i, acc):
        base = pl.multiple_of(i * CHUNK, CHUNK)
        for s in range(subs):
            here = pl.ds(base + s * SUB, SUB)
            pr = jnp.zeros((SUB, LANES), jnp.float32)
            pi = jnp.zeros((SUB, LANES), jnp.float32)
            for k in range(KRYLOV):
                vr = basis[k, here, :LANES]
                vi = basis[k, here, LANES:]
                cr, ci = weights[k], weights[k + KRYLOV]
                pr = pr + (cr * vr - ci * vi)
                pi = pi + (cr * vi + ci * vr)
            work[here, :LANES] = pr
            work[here, LANES:] = pi
            position = sub_pos + (base + s * SUB) * LANES
            occupied = lax.shift_right_logical(position, channel) & 1
            acc = acc + fold(jnp.where(occupied == 1, pr * pr + pi * pi, 0.0))
        return acc

    total = jnp.sum(lax.fori_loop(0, chunks, combine, zero_tile))
    jumped = channel < SPINS
    size = jnp.float32(rows * LANES)
    total = jnp.where(jumped, total, size)
    root = jnp.sqrt(size / jnp.full((8, LANES), total, jnp.float32))
    scale = jnp.max(root)
    in_lanes = channel < LANE_BITS
    lane_shift = jnp.where(in_lanes, lax.shift_left(1, channel), 0)
    row_shift = jnp.where(
        in_lanes | (channel >= SPINS),
        0,
        lax.shift_left(1, jnp.maximum(channel - LANE_BITS, 0)),
    )
    in_sublanes = row_shift < 8
    near = jnp.where(in_sublanes, row_shift, 0)
    far = jnp.where(in_sublanes, 0, row_shift)
    lane_turn = (LANES - lane_shift) % LANES
    row_turn = (SUB - near) % SUB

    def jump(i, carry):
        local = pl.multiple_of(i * SUB, SUB)
        base = device * block_rows + local
        source = pl.multiple_of(base + far, 8)
        position = sub_pos + base * LANES
        vacant = (lax.shift_right_logical(position, channel) & 1) == 0
        for part in range(2):
            x = work[pl.ds(source, SUB), part * LANES : (part + 1) * LANES]
            x = pltpu.roll(x, row_turn, 0)
            x = pltpu.roll(x, lane_turn, 1)
            out[part, pl.ds(local, SUB), :] = jnp.where(vacant, x * scale, 0.0)
        return carry

    lax.fori_loop(0, block_rows // SUB, jump, 0)


def body(amplitudes, couplings, fields, decays, channel):
    node_count = lax.axis_size("amp")
    local_len = amplitudes.shape[2]
    block_rows = local_len // LANES
    rows = node_count * block_rows
    vmem = pl.BlockSpec(memory_space=pltpu.VMEM)
    smem = pl.BlockSpec(memory_space=pltpu.SMEM)
    call = pl.pallas_call(
        kernel,
        out_shape=jax.ShapeDtypeStruct((2, block_rows, LANES), jnp.float32),
        in_specs=[smem] * 4 + [vmem],
        out_specs=vmem,
        scratch_shapes=[
            pltpu.VMEM((KRYLOV, rows, 2 * LANES), jnp.float32),
            pltpu.VMEM((rows + rows // 2, 2 * LANES), jnp.float32),
            pltpu.VMEM((CHUNK, 2 * LANES), jnp.float32),
            pltpu.VMEM((2, CHUNK, CHUNK), jnp.bfloat16),
            pltpu.VMEM((2, CHUNK, CHUNK), jnp.bfloat16),
            pltpu.VMEM((2, CHUNK, LANES), jnp.float32),
        ],
        compiler_params=pltpu.CompilerParams(vmem_limit_bytes=62 * 1024 * 1024),
        name="trajectory",
    )
    results = []
    for t in range(amplitudes.shape[0]):
        block = amplitudes[t].reshape(2, block_rows, LANES)
        state = lax.all_gather(block, "amp")
        results.append(call(channel[t : t + 1], couplings, fields, decays, state))
    return jnp.stack(results).reshape(amplitudes.shape)


def solution(mesh):
    placed = (P("traj", None, "amp"), P(), P(), P(), P("traj"))
    return jax.shard_map(
        body, mesh=mesh, in_specs=placed, out_specs=P("traj", None, "amp"), check_vma=False
    )
```

time: 2200 us -> 188 us (0.09); the launches traced: 2170 us -> 188 us
  local copies, waits for them, and re-layouts: 1050 us -> 5.12 us
  other arithmetic: 535 us -> 0 us
  matrix products: 433 us -> 0 us
  Pallas kernels: 0 us -> 113 us
  blocking collectives: 110 us -> 0 us
  waiting for transfers between devices: 8.11 us -> 55 us
    rev x19 -> x0, local copies, waits for them, and re-layouts: 514 us -> none  [flip_axis(): jnp.flip(tensor.reshape(new_shape), axis=axis_pos + 1).reshape(old_shape)]
    dot_general x61 -> x0, matrix products: 433 us -> none  [the longest x7 148 us: body(): jnp.einsum('tkcrl,tpcrl->tkp', stacked, paired, precision=highest)]
    reshape x43 -> x0, local copies, waits for them, and re-layouts: 317 us -> none  [the longest x19 180 us: flip_axis(): jnp.flip(tensor.reshape(new_shape), axis=axis_pos + 1).reshape(old_shape)]
    another operation x39 -> x1, local copies, waits for them, and re-layouts: 158 us -> 2.86 us  [body(): return jnp.stack(results).reshape(amplitudes.shape)]
    sub x86 -> x0, other arithmetic: 154 us -> none  [the longest x8 120 us: body(): out_imag = diag_real * imag_part + diag_imag * real_part - flipped[:, 1]]
    mul x81 -> x0, other arithmetic: 150 us -> none  [the longest x80 150 us: body(): fields[apply_spin_pos] * flip_axis(apply_vector, 2, apply_spin_pos - 7)]
    neg x9 -> x0, other arithmetic: 120 us -> none  [the longest x8 120 us: body(): swapped = jnp.stack([applied[:, 1], -applied[:, 0]], axis=1)]
    pallas_call x0 -> x1, Pallas kernels: none -> 113 us  [body(): results.append(call(channel[t:t + 1], couplings, fields, decays, state))]
  transfers between devices with their start and end apart: 18 -> 1, of which waited for: 1 -> 1; matrix products, arithmetic and copies ran while one was open for 21% -> 0% of each run, Pallas kernels for 0% -> 0%
where the time goes in v1:
time: 188 us
  Pallas kernels  113 us (60%)
  waiting for transfers between devices  55 us (29%)
  between operations  14 us (7%)
  local copies, waits for them, and re-layouts  5.12 us (3%)
    pallas_call x1, Pallas kernels, body(): results.append(call(channel[t:t + 1], couplings, fields, decays, state))  113 us
    all_gather x1, waiting for transfers between devices, body(): state = lax.all_gather(block, 'amp')  55 us
  transfers between devices with their start and end apart: 1, of which 1 were waited for; matrix products, arithmetic and copies ran while one was open for 0% of the time, Pallas kernels for 0%

profile of v1, /device:TPU:0, one launch (start us, length us, event | category | flops | bytes accessed | tf_op | source)
XLA Modules:
  0.0 187.6 jit_solution(17673568868756250610)
XLA Ops:
  6.5 0.0 all-gather.2.cloned.1.call-start
  6.5 2.3 %copy.8 = f32[1,2,1024,128]{3,2,1,0:T(8,128)} copy(f32[1,2,1024,128]{3,1,2,0:T(2,128)} %bitcast.6) | data formatting | bytes 2097152
  8.8 0.0 all-gather.2.cloned.1.call-update
  9.5 55.0 %all-gather.2.cloned.1.call-done.state = f32[4,2,1024,128]{3,2,1,0:T(8,128)} async-done(((f32[1,2,1024,128]{3,2,1,0:T(8,128)}), f32[4,2,1024,128]{3,2,1,0:T(8,128)}) %all-gather.2.cloned.1.call-update) | async-done | bytes 4194320 | tf_op jit(solution)/shard_map/all_gather | solution.py:329
  64.5 113.4 %trajectory.1 = f32[2,1024,128]{2,1,0:T(8,128)} custom-call(s32[1]{0:T(128)S(6)} %copy.9.channel_ref, f32[18]{0:T(128)} %couplings.1, f32[19]{0:T(128)} %fields.1, f32[19]{0:T(128)} %decays.1, f32[4,2,1024,128]{3,2,1,0:T(8,128)} %all-gather.2.cloned.1.call-done.state), custom_call_target="tpu_custom_call" | custom-call | tf_op jit(solution)/shard_map/trajectory/pallas_call | solution.py:330
  177.9 2.9 %reshape_stack.3 = f32[1,2,131072]{2,1,0:T(2,128)} reshape(f32[2,1024,128]{2,1,0:T(8,128)} %trajectory.1) | data formatting | bytes 2097152 | tf_op jit(solution)/shard_map/reshape;stack | solution.py:331
Async XLA Ops:
  6.5 58.0 %all-gather.2.cloned.1.call-start = ((), (), s32[]{:S(2)}) async-start(), calls=%async_computation | async-start | bytes 5242880 | tf_op jit(solution)/shard_map/all_gather | solution.py:329
Sparse Core Ops, SparseCore 0:
  9.2 55.2 all-gather.1

commit v2 on v1

--- a/solution.py
+++ b/solution.py
@@ -300,6 +300,64 @@
     lax.fori_loop(0, block_rows // SUB, jump, 0)
 
 
+def gather_kernel(block, out, send_sem, recv_sem):
+    me = lax.axis_index("amp")
+    near = (me ^ 1, me ^ 2)
+    barrier = pltpu.get_barrier_semaphore()
+    for partner in near:
+        pl.semaphore_signal(
+            barrier, inc=1, device_id={"amp": partner}, device_id_type=pl.DeviceIdType.MESH
+        )
+    pl.semaphore_wait(barrier, 2)
+
+    def copy(source, owner, part, axis, slot):
+        return pltpu.make_async_remote_copy(
+            src_ref=source,
+            dst_ref=out.at[owner, part],
+            send_sem=send_sem.at[slot],
+            recv_sem=recv_sem.at[slot],
+            device_id={"amp": near[axis]},
+            device_id_type=pl.DeviceIdType.MESH,
+        )
+
+    direct = {}
+    for turn in range(2):
+        for axis in range(2):
+            part = axis ^ turn
+            direct[axis, part] = copy(block.at[part], me, part, axis, 2 * axis + part)
+            direct[axis, part].start()
+    out[me] = block[...]
+    forwards = []
+    for axis in range(2):
+        direct[axis, axis].wait_recv()
+        owner = near[axis]
+        forward = copy(out.at[owner, axis], owner, axis, 1 - axis, 4 + axis)
+        forward.start()
+        forwards.append(forward)
+    for axis in range(2):
+        direct[axis, 1 - axis].wait_recv()
+    for forward in forwards:
+        forward.wait_recv()
+    for sent in list(direct.values()) + forwards:
+        sent.wait_send()
+
+
+def gather(block):
+    node_count = lax.axis_size("amp")
+    if node_count != 4:
+        return lax.all_gather(block, "amp")
+    vmem = pl.BlockSpec(memory_space=pltpu.VMEM)
+    return pl.pallas_call(
+        gather_kernel,
+        out_shape=jax.ShapeDtypeStruct((node_count,) + block.shape, block.dtype),
+        in_specs=[vmem],
+        out_specs=vmem,
+        scratch_shapes=[pltpu.SemaphoreType.DMA((6,)), pltpu.SemaphoreType.DMA((6,))],
+        compiler_params=pltpu.CompilerParams(collective_id=0, has_side_effects=True),
+        name="gather",
+    )(block)
+
+
 def body(amplitudes, couplings, fields, decays, channel):
     node_count = lax.axis_size("amp")
     local_len = amplitudes.shape[2]
@@ -326,7 +384,7 @@
     results = []
     for t in range(amplitudes.shape[0]):
         block = amplitudes[t].reshape(2, block_rows, LANES)
-        state = lax.all_gather(block, "amp")
+        state = gather(block)
         results.append(call(channel[t : t + 1], couplings, fields, decays, state))
     return jnp.stack(results).reshape(amplitudes.shape)
 

time: 188 us -> 161 us (0.86)
  waiting for transfers between devices: 55 us -> 0 us
  Pallas kernels: 113 us -> 155 us
  between operations: 14 us -> 0.66 us
    all_gather x1 -> x0, waiting for transfers between devices: 55 us -> none  [body(): state = lax.all_gather(block, 'amp')]
    pallas_call x0 -> x1, Pallas kernels: none -> 41.9 us  [gather(): pl.pallas_call(gather_kernel, out_shape=jax.ShapeDtypeStruct((node_count,...]
  transfers between devices with their start and end apart: 1 -> 0, of which waited for: 1 -> 0; matrix products, arithmetic and copies ran while one was open for 0% -> 0% of each run, Pallas kernels for 0% -> 0%
where the time goes in v2:
time: 161 us
  Pallas kernels  155 us (96%)
  local copies, waits for them, and re-layouts  5.12 us (3%)
    pallas_call x1, Pallas kernels, body(): results.append(call(channel[t:t + 1], couplings, fields, decays, state))  113 us
    pallas_call x1, Pallas kernels, gather(): pl.pallas_call(gather_kernel, out_shape=jax.ShapeDtypeStruct((node_count,...  41.9 us

profile of v2, /device:TPU:0, one launch (start us, length us, event | category | flops | bytes accessed | tf_op | source)
XLA Modules:
  0.0 161.0 jit_solution(3250776257495823717)
XLA Ops:
  0.7 2.3 %copy.8 = f32[1,2,1024,128]{3,2,1,0:T(8,128)} copy(f32[1,2,1024,128]{3,1,2,0:T(2,128)} %bitcast.6) | data formatting | bytes 2097152
  2.9 41.9 %gather.1.state = f32[4,2,1024,128]{3,2,1,0:T(8,128)} custom-call(f32[2,1024,128]{2,1,0:T(8,128)} %bitcast.5), custom_call_target="tpu_custom_call" | custom-call | tf_op jit(solution)/shard_map/gather/pallas_call | solution.py:350
  44.8 113.4 %trajectory.1 = f32[2,1024,128]{2,1,0:T(8,128)} custom-call(s32[1]{0:T(128)S(6)} %copy.9.channel_ref, f32[18]{0:T(128)} %couplings.1, f32[19]{0:T(128)} %fields.1, f32[19]{0:T(128)} %decays.1, f32[4,2,1024,128]{3,2,1,0:T(8,128)} %gather.1.state), custom_call_target="tpu_custom_call" | custom-call | tf_op jit(solution)/shard_map/trajectory/pallas_call | solution.py:388
  158.2 2.9 %reshape_stack.3 = f32[1,2,131072]{2,1,0:T(2,128)} reshape(f32[2,1024,128]{2,1,0:T(8,128)} %trajectory.1) | data formatting | bytes 2097152 | tf_op jit(solution)/shard_map/reshape;stack | solution.py:389
